TPU v7x, 128 devices: a whole 4x4x4 slice. The times are simulated.
128 devices in a mesh: dp: 4 (over x), fy: 4 (over z_hi, core), fx: 8 (over z_lo, y).
Axes of the slice: x: 4, y: 4, z: 4 (z_hi: 2, z_lo: 2; z = z_hi * 2 + z_lo), core: 2. Of those that a mesh axis runs over, the one named last changes fastest.
Arguments:
- fine_tokens: bfloat16 [4, 64, 256, 768], P('dp', 'fy', 'fx'), may hold values from -40 to 40
- parent: int32 [4, 64, 64], P('dp', 'fy', 'fx'), may hold values from 0 to 511, as said below
- coarse_tokens: bfloat16 [4, 512, 768], P('dp', 'fx'), may hold values from -6 to 6
- tile_level: int32 [4, 512], P('dp', 'fx'), may hold values from 0 to 2
- level_table: float32 [3, 768], replicated, may hold values from -3 to 3
- norm_gain: float32 [768], replicated, may hold values from 0.5 to 1.5
- qkv_weight: bfloat16 [768, 2304], replicated, may hold values from -7 to 7
- out_weight: bfloat16 [768, 768], replicated, may hold values from -0.21875 to 0.21875
- cotangent: bfloat16 [4, 64, 256, 768], P('dp', 'fy', 'fx'), may hold values from -6 to 6
Outputs:
- mixed: bfloat16 [4, 64, 256, 768], P('dp', 'fy', 'fx')
- grad_tokens: bfloat16 [4, 64, 256, 768], P('dp', 'fy', 'fx')
- grad_coarse: float32 [4, 512, 768], P('dp', 'fx')
- grad_qkv: float32 [768, 2304], P('dp')
- grad_out: float32 [768, 768], P('dp')
- grad_gain: float32 [768], P('dp')
- grad_level: float32 [3, 768], replicated
Inputs may be any that keep to these rules, and one draw needn't show every extreme that they name: `parent`: each entry names a coarse token of the same frame; a token of level l is drawn with weight l + 1.
All inputs are finite; a program needn't handle non-finite values.
Results may differ from a plain program's by a relative error of at most 0.025.
Values may be sent and summed in bfloat16 or wider, within the bound.
A program may use at most 128 MiB of HBM per device.

v0:
```python
import functools
import math
import jax
import jax.numpy as jnp
from jax import lax
from jax.sharding import PartitionSpec as P

HEADS = 12
BLK = 4
LEVELS = 3


def as_sent(shard):
    return jax.tree.map(lambda a: a.astype(jnp.bfloat16) if a.dtype == jnp.float32 else a, shard)


def attend_forward(queries, key_rows, values, score_scale, query_form, key_form, score_form):
    scores = (
        jnp.einsum(
            query_form + "," + key_form + "->" + score_form,
            queries,
            key_rows,
            preferred_element_type=jnp.float32,
        )
        * score_scale
    )
    weights = jax.nn.softmax(scores, axis=-1)
    rounded = weights.astype(jnp.bfloat16)
    attended = jnp.einsum(
        score_form + "," + key_form + "->" + query_form,
        rounded,
        values,
        preferred_element_type=jnp.float32,
    )
    return attended.astype(jnp.bfloat16)


def attend_grads(
    weights,
    rounded,
    queries,
    key_rows,
    values,
    grad_out,
    score_scale,
    query_form,
    key_form,
    score_form,
):
    grad_values = jnp.einsum(
        score_form + "," + query_form + "->" + key_form,
        rounded,
        grad_out,
        preferred_element_type=jnp.float32,
    ).astype(jnp.bfloat16)
    grad_weights = jnp.einsum(
        query_form + "," + key_form + "->" + score_form,
        grad_out,
        values,
        preferred_element_type=jnp.float32,
    )
    inner = jnp.sum(weights * grad_weights, axis=-1, keepdims=True)
    grad_scores = (weights * (grad_weights - inner) * score_scale).astype(jnp.bfloat16)
    grad_queries = jnp.einsum(
        score_form + "," + key_form + "->" + query_form,
        grad_scores,
        key_rows,
        preferred_element_type=jnp.float32,
    ).astype(jnp.bfloat16)
    grad_keys = jnp.einsum(
        score_form + "," + query_form + "->" + key_form,
        grad_scores,
        queries,
        preferred_element_type=jnp.float32,
    ).astype(jnp.bfloat16)
    return (grad_queries, grad_keys, grad_values)


def attend_backward(
    queries, key_rows, values, grad_out, score_scale, query_form, key_form, score_form
):
    scores = (
        jnp.einsum(
            query_form + "," + key_form + "->" + score_form,
            queries,
            key_rows,
            preferred_element_type=jnp.float32,
        )
        * score_scale
    )
    weights = jax.nn.softmax(scores, axis=-1)
    rounded = weights.astype(jnp.bfloat16)
    return attend_grads(
        weights,
        rounded,
        queries,
        key_rows,
        values,
        grad_out,
        score_scale,
        query_form,
        key_form,
        score_form,
    )


def take_rows(table_rows, row_ids):
    return jnp.take(table_rows, row_ids, axis=0)


def rows_to_batch(tensor, head_dim):
    return tensor.reshape(tensor.shape[1], tensor.shape[2], -1, head_dim)


def batch_to_rows(tensor):
    return tensor.reshape(1, tensor.shape[0], tensor.shape[1], -1)


def columns_to_batch(tensor, head_dim):
    return tensor.reshape(tensor.shape[0], tensor.shape[1], tensor.shape[3], -1, head_dim)


def batch_to_columns(tensor):
    return tensor.reshape(tensor.shape[0], tensor.shape[1], 1, tensor.shape[2], -1)


def to_row_groups(tensor, groups):
    return tensor.reshape(groups, -1, tensor.shape[2], tensor.shape[3])


def to_column_groups(tensor, groups):
    return tensor.reshape(tensor.shape[0], tensor.shape[1], groups, -1, tensor.shape[3])


def local(
    fine_tokens,
    parent,
    coarse_tokens,
    tile_level,
    level_table,
    norm_gain,
    qkv_weight,
    out_weight,
    cotangent,
):
    frame_count, row_count, column_count, model_dim = fine_tokens.shape
    row_groups = lax.axis_size("fx")
    column_groups = lax.axis_size("fy")
    owners_dev = coarse_tokens.shape[1]
    half_width = model_dim // 2
    head_dim = model_dim // HEADS
    score_scale = head_dim ** (-0.5)
    block_count = column_count // BLK
    token_shape = (frame_count, row_count, column_count, half_width)
    level_onehot = (tile_level[:, :, None] == jnp.arange(LEVELS, dtype=jnp.int32)).astype(
        jnp.float32
    )
    level_add = jnp.sum(level_onehot[:, :, :, None] * level_table[None, None, :, :], axis=2)
    summary = (coarse_tokens.astype(jnp.float32) + level_add).astype(jnp.bfloat16)
    shard_piece = lax.all_gather(summary, "fx", axis=1, tiled=True)
    piece_rows = shard_piece.shape[1]
    inside = (parent >= 0) & (parent < piece_rows)
    local_index = jnp.clip(parent, 0, piece_rows - 1)
    picked = jax.vmap(take_rows)(shard_piece, local_index)
    read_rows = jnp.where(inside[..., None], picked.astype(jnp.float32), 0.0)
    spread = jnp.broadcast_to(
        read_rows[:, :, :, None, :], (frame_count, row_count, block_count, BLK, model_dim)
    )
    residual = fine_tokens.astype(jnp.float32) + spread.reshape(
        frame_count, row_count, column_count, model_dim
    )
    inv_rms = lax.rsqrt(jnp.mean(residual * residual, axis=-1, keepdims=True) + 1e-06)
    normed_pre = residual * inv_rms
    normed = (normed_pre * norm_gain).astype(jnp.bfloat16)
    flat_normed = normed.reshape(-1, model_dim)
    projected = jnp.dot(flat_normed, qkv_weight, preferred_element_type=jnp.float32).astype(
        jnp.bfloat16
    )
    projected = projected.reshape(frame_count, row_count, column_count, 3 * model_dim)
    row_query = projected[..., 0:half_width]
    column_query = projected[..., half_width:model_dim]
    row_key = projected[..., model_dim : model_dim + half_width]
    column_key = projected[..., model_dim + half_width : 2 * model_dim]
    row_value = projected[..., 2 * model_dim : 2 * model_dim + half_width]
    column_value = projected[..., 2 * model_dim + half_width : 3 * model_dim]
    flat_cot = cotangent.reshape(-1, model_dim)
    grad_att = jnp.dot(flat_cot, out_weight.T, preferred_element_type=jnp.float32).astype(
        jnp.bfloat16
    )
    grad_att = grad_att.reshape(frame_count, row_count, column_count, model_dim)
    row_grad_out = grad_att[..., 0:half_width]
    column_grad_out = grad_att[..., half_width:model_dim]
    queries = lax.all_to_all(
        to_row_groups(row_query, row_groups), "fx", split_axis=0, concat_axis=2, tiled=True
    )
    key_rows = lax.all_to_all(
        to_row_groups(row_key, row_groups), "fx", split_axis=0, concat_axis=2, tiled=True
    )
    values = lax.all_to_all(
        to_row_groups(row_value, row_groups), "fx", split_axis=0, concat_axis=2, tiled=True
    )
    attended_rows = attend_forward(
        rows_to_batch(queries, head_dim),
        rows_to_batch(key_rows, head_dim),
        rows_to_batch(values, head_dim),
        score_scale,
        "bqhd",
        "bkhd",
        "bhqk",
    )
    row_out = lax.all_to_all(
        batch_to_rows(attended_rows), "fx", split_axis=2, concat_axis=0, tiled=True
    )
    row_out = row_out.reshape(token_shape)
    queries = lax.all_to_all(
        to_column_groups(column_query, column_groups), "fy", split_axis=2, concat_axis=1, tiled=True
    )
    key_rows = lax.all_to_all(
        to_column_groups(column_key, column_groups), "fy", split_axis=2, concat_axis=1, tiled=True
    )
    values = lax.all_to_all(
        to_column_groups(column_value, column_groups), "fy", split_axis=2, concat_axis=1, tiled=True
    )
    attended_columns = attend_forward(
        columns_to_batch(queries, head_dim),
        columns_to_batch(key_rows, head_dim),
        columns_to_batch(values, head_dim),
        score_scale,
        "fqchd",
        "fkchd",
        "fchqk",
    )
    column_out = lax.all_to_all(
        batch_to_columns(attended_columns), "fy", split_axis=1, concat_axis=2, tiled=True
    )
    column_out = column_out.reshape(token_shape)
    queries = lax.all_to_all(
        to_row_groups(row_query, row_groups), "fx", split_axis=0, concat_axis=2, tiled=True
    )
    key_rows = lax.all_to_all(
        to_row_groups(row_key, row_groups), "fx", split_axis=0, concat_axis=2, tiled=True
    )
    values = lax.all_to_all(
        to_row_groups(row_value, row_groups), "fx", split_axis=0, concat_axis=2, tiled=True
    )
    grad_rows = lax.all_to_all(
        to_row_groups(row_grad_out, row_groups), "fx", split_axis=0, concat_axis=2, tiled=True
    )
    grads = attend_backward(
        rows_to_batch(queries, head_dim),
        rows_to_batch(key_rows, head_dim),
        rows_to_batch(values, head_dim),
        rows_to_batch(grad_rows, head_dim),
        score_scale,
        "bqhd",
        "bkhd",
        "bhqk",
    )
    row_back = (
        lax.all_to_all(batch_to_rows(grads[0]), "fx", split_axis=2, concat_axis=0, tiled=True),
        lax.all_to_all(batch_to_rows(grads[1]), "fx", split_axis=2, concat_axis=0, tiled=True),
        lax.all_to_all(batch_to_rows(grads[2]), "fx", split_axis=2, concat_axis=0, tiled=True),
    )
    queries = lax.all_to_all(
        to_column_groups(column_query, column_groups), "fy", split_axis=2, concat_axis=1, tiled=True
    )
    key_rows = lax.all_to_all(
        to_column_groups(column_key, column_groups), "fy", split_axis=2, concat_axis=1, tiled=True
    )
    values = lax.all_to_all(
        to_column_groups(column_value, column_groups), "fy", split_axis=2, concat_axis=1, tiled=True
    )
    grad_columns = lax.all_to_all(
        to_column_groups(column_grad_out, column_groups),
        "fy",
        split_axis=2,
        concat_axis=1,
        tiled=True,
    )
    grads = attend_backward(
        columns_to_batch(queries, head_dim),
        columns_to_batch(key_rows, head_dim),
        columns_to_batch(values, head_dim),
        columns_to_batch(grad_columns, head_dim),
        score_scale,
        "fqchd",
        "fkchd",
        "fchqk",
    )
    column_back = (
        lax.all_to_all(batch_to_columns(grads[0]), "fy", split_axis=1, concat_axis=2, tiled=True),
        lax.all_to_all(batch_to_columns(grads[1]), "fy", split_axis=1, concat_axis=2, tiled=True),
        lax.all_to_all(batch_to_columns(grads[2]), "fy", split_axis=1, concat_axis=2, tiled=True),
    )
    attended = jnp.concatenate([row_out, column_out], axis=-1)
    flat_att = attended.reshape(-1, model_dim)
    out_proj = jnp.dot(flat_att, out_weight, preferred_element_type=jnp.float32)
    mixed = (residual + out_proj.reshape(frame_count, row_count, column_count, model_dim)).astype(
        jnp.bfloat16
    )
    grad_out_local = jnp.dot(flat_att.T, flat_cot, preferred_element_type=jnp.float32)
    pieces = []
    for which in range(3):
        pieces.append(row_back[which].reshape(token_shape))
        pieces.append(column_back[which].reshape(token_shape))
    grad_projected = jnp.concatenate(pieces, axis=-1).reshape(-1, 3 * model_dim)
    grad_normed = jnp.dot(grad_projected, qkv_weight.T, preferred_element_type=jnp.float32)
    grad_qkv_local = jnp.dot(flat_normed.T, grad_projected, preferred_element_type=jnp.float32)
    flat_pre = normed_pre.reshape(-1, model_dim)
    grad_gain_local = jnp.sum(grad_normed * flat_pre, axis=0)
    grad_pre = grad_normed * norm_gain
    flat_inv = inv_rms.reshape(-1, 1)
    grad_residual = flat_inv * (
        grad_pre - flat_pre * jnp.mean(grad_pre * flat_pre, axis=-1, keepdims=True)
    ) + flat_cot.astype(jnp.float32)
    grad_fine = grad_residual.astype(jnp.bfloat16).reshape(
        frame_count, row_count, column_count, model_dim
    )
    block_grad = (
        grad_residual.reshape(frame_count, row_count, block_count, BLK, model_dim)
        .sum(axis=3)
        .reshape(frame_count, -1, model_dim)
    )
    parent_flat = parent.reshape(frame_count, -1)
    coarse_total = owners_dev * row_groups
    segment_rows = functools.partial(jax.ops.segment_sum, num_segments=coarse_total)
    dense_sum = jax.vmap(segment_rows)(block_grad, parent_flat)
    owned_rows = jax.tree.map(
        lambda part: part.astype(jnp.float32),
        lax.psum_scatter(as_sent(dense_sum), "fx", scatter_dimension=1, tiled=True),
    )
    grad_coarse = jax.tree.map(
        lambda part: part.astype(jnp.float32), lax.psum(as_sent(owned_rows), "fy")
    )
    level_part = jnp.sum(level_onehot[:, :, :, None] * grad_coarse[:, :, None, :], axis=(0, 1))
    grad_level = lax.psum(level_part, ("dp", "fx"))
    summed = (
        lax.psum(grad_qkv_local.astype(jnp.bfloat16), ("fy", "fx")).astype(jnp.float32),
        lax.psum(grad_out_local.astype(jnp.bfloat16), ("fy", "fx")).astype(jnp.float32),
        lax.psum(grad_gain_local.astype(jnp.bfloat16), ("fy", "fx")).astype(jnp.float32),
    )
    shares = (
        lax.psum_scatter(
            summed[0].astype(jnp.bfloat16), "dp", scatter_dimension=0, tiled=True
        ).astype(jnp.float32),
        lax.psum_scatter(
            summed[1].astype(jnp.bfloat16), "dp", scatter_dimension=0, tiled=True
        ).astype(jnp.float32),
        lax.psum_scatter(
            summed[2].astype(jnp.bfloat16), "dp", scatter_dimension=0, tiled=True
        ).astype(jnp.float32),
    )
    total_tokens = (
        frame_count * row_count * column_count * lax.axis_size("dp") * column_groups * row_groups
    )
    grad_scale = 1.0 / math.sqrt(total_tokens)
    return (
        mixed,
        grad_fine,
        grad_coarse,
        shares[0] * grad_scale,
        shares[1] * grad_scale,
        shares[2] * grad_scale,
        grad_level * grad_scale,
    )


def solution(mesh):
    return jax.shard_map(
        local,
        mesh=mesh,
        in_specs=(
            P("dp", "fy", "fx", None),
            P("dp", "fy", "fx"),
            P("dp", "fx", None),
            P("dp", "fx"),
            P(),
            P(),
            P(),
            P(),
            P("dp", "fy", "fx", None),
        ),
        out_specs=(
            P("dp", "fy", "fx", None),
            P("dp", "fy", "fx", None),
            P("dp", "fx", None),
            P("dp", None),
            P("dp", None),
            P("dp"),
            P(),
        ),
        check_vma=False,
    )
```

profile of v0, /device:TPU:0, one launch (start us, length us, event | category | flops | bytes accessed | tf_op | source)
XLA Modules:
  0.0 606.6 jit_solution(17159746881032802387)
XLA Ops:
  12.2 5.3 all-to-all-start.10
  23.4 31.8 %all_gather.3 = bf16[1,512,768]{2,1,0:T(8,128)(2,1)} all-gather(bf16[1,64,768]{2,1,0:T(8,128)(2,1)S(1)} %fusion.66), channel_id=1, replica_groups=mesh['dp'=4,'fy'=4,'fx'=8] {'fx'}, dimensions={1}, use_global_device_ids=true | all-gather | bytes 884736 | tf_op jit(solution)/shard_map/all_gather | solution.py:160
  55.2 2.8 gather_fusion
  60.5 2.8 broadcast_in_dim.39
  71.1 5.4 all-to-all-start.6
  78.3 7.2 %all-to-all-done.6 = bf16[1,16,4,8,384]{4,3,1,0,2:T(8,128)(2,1)} async-done(((bf16[1,16,4,8,384]{4,3,1,0,2:T(8,128)(2,1)}), bf16[1,16,4,8,384]{4,3,1,0,2:T(8,128)(2,1)}, u32[]{:S(2)}, u32[]{:S(2)}) %all-to-all-start.6) | async-done | bytes 393248 | tf_op jit(solution)/shard_map/all_to_all | solution.py:218
  85.5 4.1 all-to-all-start.5
  91.4 7.2 %all-to-all-done.5 = bf16[1,16,4,8,384]{4,3,1,0,2:T(8,128)(2,1)} async-done(((bf16[1,16,4,8,384]{4,3,1,0,2:T(8,128)(2,1)}), bf16[1,16,4,8,384]{4,3,1,0,2:T(8,128)(2,1)}, u32[]{:S(2)}, u32[]{:S(2)}) %all-to-all-start.5) | async-done | bytes 393248 | tf_op jit(solution)/shard_map/all_to_all | solution.py:215
  98.6 13.2 %all_to_all.270 = bf16[1,16,4,8,384]{4,3,1,0,2:T(8,128)(2,1)} all-to-all(bf16[1,16,4,8,384]{4,3,1,0,2:T(8,128)(2,1)} %copy.222), channel_id=1, replica_groups=mesh['dp'=4,'fy'=4,'fx'=8] {'fy'}, dimensions={2} | all-to-all | bytes 786432 | tf_op jit(solution)/shard_map/all_to_all | solution.py:221
  111.8 12.7 %all_to_all.271 = bf16[8,2,32,384]{3,2,1,0:T(8,128)(2,1)} all-to-all(bf16[8,2,32,384]{3,2,1,0:T(8,128)(2,1)} %bitcast.260), channel_id=1, replica_groups=mesh['dp'=4,'fy'=4,'fx'=8] {'fx'}, dimensions={0} | all-to-all | bytes 786432 | tf_op jit(solution)/shard_map/all_to_all | solution.py:246
  124.5 11.1 %all_to_all.272 = bf16[8,2,32,384]{3,2,1,0:T(8,128)(2,1)} all-to-all(bf16[8,2,32,384]{3,2,1,0:T(8,128)(2,1)S(1)} %bitcast.251), channel_id=1, replica_groups=mesh['dp'=4,'fy'=4,'fx'=8] {'fx'}, dimensions={0} | all-to-all | bytes 786432 | tf_op jit(solution)/shard_map/all_to_all | solution.py:196
  135.6 4.1 all-to-all-start.1
  157.4 3.3 fusion.59
  160.7 6.1 %all-to-all-start = ((bf16[8,2,32,384]{3,2,1,0:T(8,128)(2,1)}), bf16[8,2,32,384]{3,2,1,0:T(8,128)(2,1)}, u32[]{:S(2)}, u32[]{:S(2)}) async-start(bf16[8,2,32,384]{3,2,1,0:T(8,128)(2,1)} %bitcast.249), calls=%async_computation | async-start | bytes 786432 | tf_op jit(solution)/shard_map/all_to_all | solution.py:199
  166.9 4.0 fusion.89
  170.8 4.6 fusion.37
  177.6 4.1 all-to-all-start.11
  181.8 3.0 convolution_convert_fusion.2
  187.0 4.6 fusion.40
  196.6 3.0 reshape.446
  199.6 2.7 copy.279
  202.4 3.0 reshape.443
  205.4 2.7 copy.280
  208.1 3.0 reshape.444
  211.1 2.7 copy.281
  213.9 3.0 reshape.445
  216.9 4.8 all-to-all-start.13
  221.7 4.5 fusion.90
  226.2 4.5 all-to-all-done.13
  230.7 4.1 all-to-all-start.15
  234.8 3.3 convolution_convert_fusion.4
  240.1 3.7 all-to-all-done.15
  243.8 5.9 all-to-all-start.14
  249.7 3.4 fusion.91
  253.1 6.6 %fusion.43 = bf16[2,6,64,256]{3,2,1,0:T(8,128)(2,1)} fusion(bf16[2,256,6,64]{1,3,2,0:T(8,128)(2,1)} %reshape.445, f32[2,6,256,256]{2,3,1,0:T(8,128)} %fusion.91, f32[2,6,256,256]{2,3,1,0:T(8,128)} %get-tuple-element.28, f32[2,6,256]{2,1,0:T(8,128)} %get-tuple-element.27), kind=kOutput, calls=%fused_computation.49 | convolution fusion | flops 106368256 | bytes 7090176 | tf_op jit(solution)/shard_map/bhqk,bkhd->bqhd/dot_general | solution.py:64
  261.6 5.7 all-to-all-start.9
  267.3 6.6 %fusion.46 = bf16[2,6,64,256]{3,2,1,0:T(8,128)(2,1)} fusion(bf16[2,256,6,64]{1,3,2,0:T(8,128)(2,1)} %reshape.444, f32[2,6,256,256]{2,3,1,0:T(8,128)} %fusion.91, f32[2,6,256,256]{2,3,1,0:T(8,128)} %get-tuple-element.28, f32[2,6,256]{2,1,0:T(8,128)} %get-tuple-element.27), kind=kOutput, calls=%fused_computation.50 | convolution fusion | flops 106368256 | bytes 7090176 | tf_op jit(solution)/shard_map/bhqk,bqhd->bkhd/dot_general | solution.py:70
  275.8 5.7 all-to-all-start.12
  307.3 3.5 all-to-all-start.7
  314.2 6.9 %all-to-all-done.7 = bf16[1,64,1,8,384]{4,3,2,0,1:T(8,128)(2,1)S(1)} async-done(((bf16[1,64,1,8,384]{4,3,2,0,1:T(8,128)(2,1)}), bf16[1,64,1,8,384]{4,3,2,0,1:T(8,128)(2,1)S(1)}, u32[]{:S(2)}, u32[]{:S(2)}) %all-to-all-start.7) | async-done | bytes 393248 | tf_op jit(solution)/shard_map/all_to_all | solution.py:233
  321.1 5.1 all-to-all-start.3
  326.3 9.3 %all-to-all-done.3 = bf16[1,2,256,384]{3,1,0,2:T(2,128)(2,1)S(1)} async-done(((bf16[1,2,256,384]{3,1,0,2:T(2,128)(2,1)}), bf16[1,2,256,384]{3,1,0,2:T(2,128)(2,1)S(1)}, u32[]{:S(2)}, u32[]{:S(2)}) %all-to-all-start.3) | async-done | bytes 393248 | tf_op jit(solution)/shard_map/all_to_all | solution.py:211
  337.6 6.4 %reduce-scatter.4.cloned.1.call-done = bf16[1,64,768]{2,1,0:T(8,128)(2,1)} async-done(((bf16[1,512,768]{2,1,0:T(8,128)(2,1)}), bf16[1,64,768]{2,1,0:T(8,128)(2,1)}) %reduce-scatter.4.cloned.1.call-update) | async-done | bytes 98320 | tf_op jit(solution)/shard_map/reduce_scatter | solution.py:330
  352.4 5.5 bitcast_convert_fusion
  359.8 10.5 %all-reduce = bf16[768]{0:T(1024)(128)(2,1)S(1)} all-reduce(bf16[768]{0:T(1024)(128)(2,1)S(1)} %get-tuple-element.7), channel_id=5, replica_groups=mesh['dp'=4,'fy'=4,'fx'=8] {'dp'}, use_global_device_ids=true, to_apply=%region_19.20.clone | all-reduce | flops 768 | bytes 3072
  370.4 62.7 %psum.42 = bf16[192]{0:T(256)(128)(2,1)S(1)} all-reduce(bf16[192]{0:T(256)(128)(2,1)S(1)} %dynamic-slice.1), channel_id=1, replica_groups=mesh['dp'=4,'fy'=4,'fx'=8] {'fy','fx'}, use_global_device_ids=true, to_apply=%region_18.19 | all-reduce | flops 192 | bytes 768 | tf_op jit(solution)/shard_map/psum | solution.py:340
  433.7 2.9 fusion.23
  439.3 154.4 %psum.39 = f32[3,768]{1,0:T(4,128)S(1)} all-reduce(f32[3,768]{1,0:T(4,128)S(1)} %multiply_reduce_fusion.4), channel_id=1, replica_groups=mesh['dp'=4,'fy'=4,'fx'=8] {'dp','fx'}, use_global_device_ids=true, to_apply=%region_21.22 | all-reduce | flops 2304 | bytes 18432 | tf_op jit(solution)/shard_map/psum | solution.py:336
  (169 shorter events, 106.0 us)
Async XLA Ops:
  8.0 59.0 %copy-start = (bf16[768,2304]{1,0:T(8,128)(2,1)S(1)}, bf16[768,2304]{1,0:T(8,128)(2,1)}, u32[]{:S(2)}) copy-start(bf16[768,2304]{1,0:T(8,128)(2,1)} %param.15) | copy-start | bytes 10616836
  10.5 7.0 %copy-start.23 = (s32[1,16,8]{1,2,0:T(8,128)S(1)}, s32[1,16,8]{1,2,0:T(8,128)}, u32[]{:S(2)}) copy-start(s32[1,16,8]{1,2,0:T(8,128)} %param.10) | copy-start | bytes 1540
  10.5 7.5 %copy-start.27 = (s32[1,64]{1,0:T(1,128)S(1)}, s32[1,64]{1,0:T(1,128)}, u32[]{:S(2)}) copy-start(s32[1,64]{1,0:T(1,128)} %param.12) | copy-start | bytes 772
  12.2 58.9 %all-to-all-start.10 = ((bf16[1,16,4,8,384]{4,3,1,0,2:T(8,128)(2,1)}), bf16[1,16,4,8,384]{4,3,1,0,2:T(8,128)(2,1)}, u32[]{:S(2)}, u32[]{:S(2)}) async-start(bf16[1,16,4,8,384]{4,3,1,0,2:T(8,128)(2,1)} %copy.239), calls=%async_computation.10 | async-start | bytes 786432 | tf_op jit(solution)/shard_map/all_to_all | solution.py:273
  63.3 2.1 copy-start.2
  63.3 2.3 copy-start.12
  63.3 2.3 copy-start.25
  67.0 2.0 copy-start.21
  71.1 14.4 %all-to-all-start.6 = ((bf16[1,16,4,8,384]{4,3,1,0,2:T(8,128)(2,1)}), bf16[1,16,4,8,384]{4,3,1,0,2:T(8,128)(2,1)}, u32[]{:S(2)}, u32[]{:S(2)}) async-start(bf16[1,16,4,8,384]{4,3,1,0,2:T(8,128)(2,1)} %copy.224), calls=%async_computation.6 | async-start | bytes 786432 | tf_op jit(solution)/shard_map/all_to_all | solution.py:218
  85.5 13.1 %all-to-all-start.5 = ((bf16[1,16,4,8,384]{4,3,1,0,2:T(8,128)(2,1)}), bf16[1,16,4,8,384]{4,3,1,0,2:T(8,128)(2,1)}, u32[]{:S(2)}, u32[]{:S(2)}) async-start(bf16[1,16,4,8,384]{4,3,1,0,2:T(8,128)(2,1)} %copy.223), calls=%async_computation.5 | async-start | bytes 786432 | tf_op jit(solution)/shard_map/all_to_all | solution.py:215
  98.6 25.9 %copy-start.14 = (bf16[1,16,32,384]{3,2,1,0:T(8,128)(2,1)S(1)}, bf16[1,16,32,384]{3,2,1,0:T(8,128)(2,1)}, u32[]{:S(2)}) copy-start(bf16[1,16,32,384]{3,2,1,0:T(8,128)(2,1)} %get-tuple-element.15) | copy-start | bytes 1179652
  135.6 25.2 %all-to-all-start.1 = ((bf16[8,2,32,384]{3,2,1,0:T(8,128)(2,1)}), bf16[8,2,32,384]{3,2,1,0:T(8,128)(2,1)}, u32[]{:S(2)}, u32[]{:S(2)}) async-start(bf16[8,2,32,384]{3,2,1,0:T(8,128)(2,1)} %bitcast.250), calls=%async_computation.1 | async-start | bytes 786432 | tf_op jit(solution)/shard_map/all_to_all | solution.py:193
  160.7 16.9 %all-to-all-start = ((bf16[8,2,32,384]{3,2,1,0:T(8,128)(2,1)}), bf16[8,2,32,384]{3,2,1,0:T(8,128)(2,1)}, u32[]{:S(2)}, u32[]{:S(2)}) async-start(bf16[8,2,32,384]{3,2,1,0:T(8,128)(2,1)} %bitcast.249), calls=%async_computation | async-start | bytes 786432 | tf_op jit(solution)/shard_map/all_to_all | solution.py:199
  177.6 39.3 %all-to-all-start.11 = ((bf16[1,64,1,8,384]{4,3,2,0,1:T(8,128)(2,1)}), bf16[1,64,1,8,384]{4,3,2,0,1:T(8,128)(2,1)}, u32[]{:S(2)}, u32[]{:S(2)}) async-start(bf16[1,64,1,8,384]{4,3,2,0,1:T(8,128)(2,1)} %copy.244), calls=%async_computation.11 | async-start | bytes 786432 | tf_op jit(solution)/shard_map/all_to_all | solution.py:291
  216.9 13.8 %all-to-all-start.13 = ((bf16[1,64,1,8,384]{4,3,2,0,1:T(8,128)(2,1)}), bf16[1,64,1,8,384]{4,3,2,0,1:T(8,128)(2,1)}, u32[]{:S(2)}, u32[]{:S(2)}) async-start(bf16[1,64,1,8,384]{4,3,2,0,1:T(8,128)(2,1)} %copy.253), calls=%async_computation.13 | async-start | bytes 786432 | tf_op jit(solution)/shard_map/all_to_all | solution.py:292
  230.7 13.1 %all-to-all-start.15 = ((bf16[1,64,1,8,384]{4,3,2,0,1:T(8,128)(2,1)}), bf16[1,64,1,8,384]{4,3,2,0,1:T(8,128)(2,1)}, u32[]{:S(2)}, u32[]{:S(2)}) async-start(bf16[1,64,1,8,384]{4,3,2,0,1:T(8,128)(2,1)} %copy.262), calls=%async_computation.15 | async-start | bytes 786432 | tf_op jit(solution)/shard_map/all_to_all | solution.py:293
  243.8 17.8 %all-to-all-start.14 = ((bf16[1,2,256,384]{3,1,0,2:T(2,128)(2,1)}), bf16[1,2,256,384]{3,1,0,2:T(2,128)(2,1)}, u32[]{:S(2)}, u32[]{:S(2)}) async-start(bf16[1,2,256,384]{3,1,0,2:T(2,128)(2,1)} %copy.257), calls=%async_computation.14 | async-start | bytes 786432 | tf_op jit(solution)/shard_map/all_to_all | solution.py:262
  261.6 14.2 %all-to-all-start.9 = ((bf16[1,2,256,384]{3,1,0,2:T(2,128)(2,1)}), bf16[1,2,256,384]{3,1,0,2:T(2,128)(2,1)}, u32[]{:S(2)}, u32[]{:S(2)}) async-start(bf16[1,2,256,384]{3,1,0,2:T(2,128)(2,1)} %copy.236), calls=%async_computation.9 | async-start | bytes 786432 | tf_op jit(solution)/shard_map/all_to_all | solution.py:260
  275.8 16.9 %all-to-all-start.12 = ((bf16[1,2,256,384]{3,1,0,2:T(2,128)(2,1)}), bf16[1,2,256,384]{3,1,0,2:T(2,128)(2,1)}, u32[]{:S(2)}, u32[]{:S(2)}) async-start(bf16[1,2,256,384]{3,1,0,2:T(2,128)(2,1)} %copy.248), calls=%async_computation.12 | async-start | bytes 786432 | tf_op jit(solution)/shard_map/all_to_all | solution.py:261
  281.6 62.5 %reduce-scatter.4.cloned.1.call-start = ((), (), s32[]{:S(2)}) async-start(), calls=%async_computation.19 | async-start | bytes 884736 | tf_op jit(solution)/shard_map/reduce_scatter | solution.py:330
  292.7 1.2 copy-start.9
  292.7 1.3 copy-start.17
  293.8 1.1 copy-start.16
  293.9 1.1 copy-start.7
  293.9 1.2 copy-start.5
  294.0 1.2 copy-start.15
  294.1 1.7 copy-start.4
  294.1 1.7 copy-start.26
  295.8 2.2 copy-start.19
  302.6 1.5 copy-start.11
  302.6 1.5 copy-start.24
  306.2 4.6 copy-start.18
  306.2 4.6 copy-start.29
  307.3 13.8 %all-to-all-start.7 = ((bf16[1,64,1,8,384]{4,3,2,0,1:T(8,128)(2,1)}), bf16[1,64,1,8,384]{4,3,2,0,1:T(8,128)(2,1)S(1)}, u32[]{:S(2)}, u32[]{:S(2)}) async-start(bf16[1,64,1,8,384]{4,3,2,0,1:T(8,128)(2,1)} %copy.229), calls=%async_computation.7 | async-start | bytes 786432 | tf_op jit(solution)/shard_map/all_to_all | solution.py:233
  314.2 21.5 %copy-start.20 = (bf16[1,16,32,768]{3,2,1,0:T(8,128)(2,1)S(1)}, bf16[1,16,32,768]{3,2,1,0:T(8,128)(2,1)}, u32[]{:S(2)}) copy-start(bf16[1,16,32,768]{3,2,1,0:T(8,128)(2,1)} %param.17) | copy-start | bytes 2359300
  321.1 14.5 %all-to-all-start.3 = ((bf16[1,2,256,384]{3,1,0,2:T(2,128)(2,1)}), bf16[1,2,256,384]{3,1,0,2:T(2,128)(2,1)S(1)}, u32[]{:S(2)}, u32[]{:S(2)}) async-start(bf16[1,2,256,384]{3,1,0,2:T(2,128)(2,1)} %copy.219), calls=%async_computation.3 | async-start | bytes 786432 | tf_op jit(solution)/shard_map/all_to_all | solution.py:211
  326.2 110.4 %all-reduce.5.cloned.1.call-start = ((), (), s32[]{:S(2)}) async-start(), calls=%async_computation.20 | async-start | bytes 196608 | tf_op jit(solution)/shard_map/psum | solution.py:333
  335.8 8.3 %copy-start.10 = (bf16[8,1,2,32,384]{4,3,2,0,1:T(8,128)(2,1)S(1)}, bf16[8,1,2,32,384]{4,3,2,0,1:T(8,128)(2,1)}, u32[]{:S(2)}) copy-start(bf16[8,1,2,32,384]{4,3,2,0,1:T(8,128)(2,1)} %copy.238) | copy-start | bytes 1179652
  337.6 9.5 %copy-start.8 = (bf16[8,1,2,32,384]{4,3,2,0,1:T(8,128)(2,1)S(1)}, bf16[8,1,2,32,384]{4,3,2,0,1:T(8,128)(2,1)}, u32[]{:S(2)}) copy-start(bf16[8,1,2,32,384]{4,3,2,0,1:T(8,128)(2,1)} %copy-done.7) | copy-start | bytes 1179652
  344.0 94.2 %reduce-scatter.8.cloned.1.call-start = ((), (), s32[]{:S(2)}) async-start(), calls=%async_computation.22 | async-start | bytes 1474560 | tf_op jit(solution)/shard_map/reduce_scatter | solution.py:346
  345.0 4.8 copy-start.6
  345.0 93.2 %reduce-scatter.6.cloned.1.call-start = ((), (), s32[]{:S(2)}) async-start(), calls=%async_computation.21 | async-start | bytes 4423680 | tf_op jit(solution)/shard_map/reduce_scatter | solution.py:343
  347.1 5.3 copy-start.22
  357.9 0.7 copy-start.28
  357.9 75.8 %copy-start.3 = (f32[1,16,32,768]{3,2,1,0:T(8,128)S(1)}, f32[1,16,32,768]{3,2,1,0:T(8,128)}, u32[]{:S(2)}) copy-start(f32[1,16,32,768]{3,2,1,0:T(8,128)} %broadcast_in_dim.39) | copy-start | bytes 4718596
  357.9 75.8 %copy-start.13 = (bf16[1,16,32,768]{3,2,1,0:T(8,128)(2,1)S(1)}, bf16[1,16,32,768]{3,2,1,0:T(8,128)(2,1)}, u32[]{:S(2)}) copy-start(bf16[1,16,32,768]{3,2,1,0:T(8,128)(2,1)} %param.9) | copy-start | bytes 2359300
  357.9 236.4 %all-reduce.7.cloned.1.call-start = ((), (), s32[]{:S(2)}) async-start(), calls=%async_computation.23 | async-start | bytes 2359296 | tf_op jit(solution)/shard_map/psum | solution.py:338
  594.3 4.5 copy-start.1
Sparse Core Ops, SparseCore 0:
  303.7 40.2 reduce-scatter.3
  346.5 38.8 all-reduce.4
Sparse Core Ops, SparseCore 1:
  347.5 23.0 reduce-scatter.7
  372.9 41.1 reduce-scatter.5
  438.3 101.2 all-reduce.6
where the time goes:
time: 618 us; the launch traced here: 607 us
  blocking collectives  296 us (48%)
  local copies, waits for them, and re-layouts  97.6 us (16%)
  matrix products  65.2 us (11%)
  starting transfers between devices  64.2 us (10%)
  waiting for transfers between devices  45.4 us (7%)
  other arithmetic  20.7 us (3%)
  between operations  17 us (3%)
    psum x1, blocking collectives, local(): grad_level = lax.psum(level_part, ('dp', 'fx'))  154 us
    psum x1, blocking collectives, local(): lax.psum(grad_gain_local.astype(jnp.bfloat16), ('fy', 'fx'))  62.7 us
    all_gather x1, blocking collectives, local(): shard_piece = lax.all_gather(summary, 'fx', axis=1, tiled=True)  31.8 us
    reshape x8, local copies, waits for them, and re-layouts, rows_to_batch(): return tensor.reshape(tensor.shape[1], tensor.shape[2], -1, head_dim)  23 us
    another operation x7, local copies, waits for them, and re-layouts  17.7 us
    all_to_all x1, blocking collectives, local(): lax.all_to_all(to_column_groups(column_value, column_groups), 'fy', split...  13.2 us
    all_to_all x1, blocking collectives, local(): lax.all_to_all(to_row_groups(row_grad_out, row_groups), 'fx', split_axis=...  12.7 us
  transfers between devices with their start and end apart: 18, of which 7 were waited for; matrix products, arithmetic and copies ran while one was open for 27% of the time, Pallas kernels for 0%

commit v1 on v0

--- a/solution.py
+++ b/solution.py
@@ -333,7 +333,7 @@
         lambda part: part.astype(jnp.float32), lax.psum(as_sent(owned_rows), "fy")
     )
     level_part = jnp.sum(level_onehot[:, :, :, None] * grad_coarse[:, :, None, :], axis=(0, 1))
-    grad_level = lax.psum(level_part, ("dp", "fx"))
+    grad_level = lax.psum(lax.psum(level_part, "dp"), "fx")
     summed = (
         lax.psum(grad_qkv_local.astype(jnp.bfloat16), ("fy", "fx")).astype(jnp.float32),
         lax.psum(grad_out_local.astype(jnp.bfloat16), ("fy", "fx")).astype(jnp.float32),

time: 618 us -> 563 us (0.911)
  the two profiles are of different devices: /device:TPU:0 before, /device:TPU:1 now
where the time goes in v1:
time: 563 us; the launch traced here: 552 us
  blocking collectives  170 us (30%)
  waiting for transfers between devices  105 us (19%)
  local copies, waits for them, and re-layouts  97.7 us (17%)
  starting transfers between devices  76.6 us (14%)
  matrix products  65.2 us (12%)
  other arithmetic  20.7 us (4%)
  between operations  17 us (3%)
    psum x1, waiting for transfers between devices, local(): lax.psum(grad_qkv_local.astype(jnp.bfloat16), ('fy', 'fx'))  70 us
    psum x1, blocking collectives, local(): lax.psum(grad_gain_local.astype(jnp.bfloat16), ('fy', 'fx'))  64.7 us
    psum x2, blocking collectives, local(): grad_level = lax.psum(lax.psum(level_part, 'dp'), 'fx')  34.5 us
    all_gather x1, blocking collectives, local(): shard_piece = lax.all_gather(summary, 'fx', axis=1, tiled=True)  26.4 us
    reshape x8, local copies, waits for them, and re-layouts, rows_to_batch(): return tensor.reshape(tensor.shape[1], tensor.shape[2], -1, head_dim)  23.1 us
    another operation x7, local copies, waits for them, and re-layouts  17.8 us
    all_to_all x1, blocking collectives, local(): lax.all_to_all(to_column_groups(column_value, column_groups), 'fy', split...  13.1 us
    all_to_all x1, blocking collectives, local(): lax.all_to_all(to_row_groups(row_grad_out, row_groups), 'fx', split_axis=...  11.8 us
  transfers between devices with their start and end apart: 18, of which 8 were waited for; matrix products, arithmetic and copies ran while one was open for 29% of the time, Pallas kernels for 0%

profile of v1, /device:TPU:1, one launch (start us, length us, event | category | flops | bytes accessed | tf_op | source)
XLA Modules:
  0.0 552.4 jit_solution(13026054582719284484)
XLA Ops:
  12.2 6.6 %all-to-all-start.10 = ((bf16[1,16,4,8,384]{4,3,1,0,2:T(8,128)(2,1)}), bf16[1,16,4,8,384]{4,3,1,0,2:T(8,128)(2,1)}, u32[]{:S(2)}, u32[]{:S(2)}) async-start(bf16[1,16,4,8,384]{4,3,1,0,2:T(8,128)(2,1)} %copy.239), calls=%async_computation.10 | async-start | bytes 786432 | tf_op jit(solution)/shard_map/all_to_all | solution.py:273
  24.7 26.4 %all_gather.3 = bf16[1,512,768]{2,1,0:T(8,128)(2,1)} all-gather(bf16[1,64,768]{2,1,0:T(8,128)(2,1)S(1)} %fusion.66), channel_id=1, replica_groups=mesh['dp'=4,'fy'=4,'fx'=8] {'fx'}, dimensions={1}, use_global_device_ids=true | all-gather | bytes 884736 | tf_op jit(solution)/shard_map/all_gather | solution.py:160
  51.1 2.7 gather_fusion
  56.5 2.8 broadcast_in_dim.39
  67.1 10.8 %all-to-all-start.6 = ((bf16[1,16,4,8,384]{4,3,1,0,2:T(8,128)(2,1)}), bf16[1,16,4,8,384]{4,3,1,0,2:T(8,128)(2,1)}, u32[]{:S(2)}, u32[]{:S(2)}) async-start(bf16[1,16,4,8,384]{4,3,1,0,2:T(8,128)(2,1)} %copy.224), calls=%async_computation.6 | async-start | bytes 786432 | tf_op jit(solution)/shard_map/all_to_all | solution.py:218
  79.7 6.3 %all-to-all-done.6 = bf16[1,16,4,8,384]{4,3,1,0,2:T(8,128)(2,1)} async-done(((bf16[1,16,4,8,384]{4,3,1,0,2:T(8,128)(2,1)}), bf16[1,16,4,8,384]{4,3,1,0,2:T(8,128)(2,1)}, u32[]{:S(2)}, u32[]{:S(2)}) %all-to-all-start.6) | async-done | bytes 393248 | tf_op jit(solution)/shard_map/all_to_all | solution.py:218
  85.9 5.0 all-to-all-start.5
  92.8 6.3 %all-to-all-done.5 = bf16[1,16,4,8,384]{4,3,1,0,2:T(8,128)(2,1)} async-done(((bf16[1,16,4,8,384]{4,3,1,0,2:T(8,128)(2,1)}), bf16[1,16,4,8,384]{4,3,1,0,2:T(8,128)(2,1)}, u32[]{:S(2)}, u32[]{:S(2)}) %all-to-all-start.5) | async-done | bytes 393248 | tf_op jit(solution)/shard_map/all_to_all | solution.py:215
  99.0 13.1 %all_to_all.270 = bf16[1,16,4,8,384]{4,3,1,0,2:T(8,128)(2,1)} all-to-all(bf16[1,16,4,8,384]{4,3,1,0,2:T(8,128)(2,1)} %copy.222), channel_id=1, replica_groups=mesh['dp'=4,'fy'=4,'fx'=8] {'fy'}, dimensions={2} | all-to-all | bytes 786432 | tf_op jit(solution)/shard_map/all_to_all | solution.py:221
  112.2 11.8 %all_to_all.271 = bf16[8,2,32,384]{3,2,1,0:T(8,128)(2,1)} all-to-all(bf16[8,2,32,384]{3,2,1,0:T(8,128)(2,1)} %bitcast.260), channel_id=1, replica_groups=mesh['dp'=4,'fy'=4,'fx'=8] {'fx'}, dimensions={0} | all-to-all | bytes 786432 | tf_op jit(solution)/shard_map/all_to_all | solution.py:246
  124.0 10.2 %all_to_all.272 = bf16[8,2,32,384]{3,2,1,0:T(8,128)(2,1)} all-to-all(bf16[8,2,32,384]{3,2,1,0:T(8,128)(2,1)S(1)} %bitcast.251), channel_id=1, replica_groups=mesh['dp'=4,'fy'=4,'fx'=8] {'fx'}, dimensions={0} | all-to-all | bytes 786432 | tf_op jit(solution)/shard_map/all_to_all | solution.py:196
  134.2 4.1 all-to-all-start.1
  156.1 3.3 fusion.59
  159.4 5.6 %all-to-all-start = ((bf16[8,2,32,384]{3,2,1,0:T(8,128)(2,1)}), bf16[8,2,32,384]{3,2,1,0:T(8,128)(2,1)}, u32[]{:S(2)}, u32[]{:S(2)}) async-start(bf16[8,2,32,384]{3,2,1,0:T(8,128)(2,1)} %bitcast.249), calls=%async_computation | async-start | bytes 786432 | tf_op jit(solution)/shard_map/all_to_all | solution.py:199
  165.0 3.9 fusion.89
  168.9 4.6 fusion.37
  175.7 7.4 %all-to-all-start.11 = ((bf16[1,64,1,8,384]{4,3,2,0,1:T(8,128)(2,1)}), bf16[1,64,1,8,384]{4,3,2,0,1:T(8,128)(2,1)}, u32[]{:S(2)}, u32[]{:S(2)}) async-start(bf16[1,64,1,8,384]{4,3,2,0,1:T(8,128)(2,1)} %copy.244), calls=%async_computation.11 | async-start | bytes 786432 | tf_op jit(solution)/shard_map/all_to_all | solution.py:291
  183.1 3.0 convolution_convert_fusion.2
  188.4 4.6 fusion.40
  195.2 2.7 copy.283
  198.0 3.0 reshape.446
  203.8 3.0 reshape.443
  209.5 3.0 reshape.444
  215.3 3.0 reshape.445
  218.3 4.8 all-to-all-start.13
  223.1 4.5 fusion.90
  227.6 3.5 all-to-all-done.13
  231.2 5.0 all-to-all-start.15
  236.2 3.3 convolution_convert_fusion.4
  241.5 2.8 all-to-all-done.15
  244.3 5.7 %all-to-all-start.14 = ((bf16[1,2,256,384]{3,1,0,2:T(2,128)(2,1)}), bf16[1,2,256,384]{3,1,0,2:T(2,128)(2,1)}, u32[]{:S(2)}, u32[]{:S(2)}) async-start(bf16[1,2,256,384]{3,1,0,2:T(2,128)(2,1)} %copy.257), calls=%async_computation.14 | async-start | bytes 786432 | tf_op jit(solution)/shard_map/all_to_all | solution.py:262
  249.9 3.4 fusion.91
  253.3 6.6 %fusion.43 = bf16[2,6,64,256]{3,2,1,0:T(8,128)(2,1)} fusion(bf16[2,256,6,64]{1,3,2,0:T(8,128)(2,1)} %reshape.445, f32[2,6,256,256]{2,3,1,0:T(8,128)} %fusion.91, f32[2,6,256,256]{2,3,1,0:T(8,128)} %get-tuple-element.28, f32[2,6,256]{2,1,0:T(8,128)} %get-tuple-element.27), kind=kOutput, calls=%fused_computation.49 | convolution fusion | flops 106368256 | bytes 7090176 | tf_op jit(solution)/shard_map/bhqk,bkhd->bqhd/dot_general | solution.py:64
  261.8 5.1 all-to-all-start.9
  267.0 6.6 %fusion.46 = bf16[2,6,64,256]{3,2,1,0:T(8,128)(2,1)} fusion(bf16[2,256,6,64]{1,3,2,0:T(8,128)(2,1)} %reshape.444, f32[2,6,256,256]{2,3,1,0:T(8,128)} %fusion.91, f32[2,6,256,256]{2,3,1,0:T(8,128)} %get-tuple-element.28, f32[2,6,256]{2,1,0:T(8,128)} %get-tuple-element.27), kind=kOutput, calls=%fused_computation.50 | convolution fusion | flops 106368256 | bytes 7090176 | tf_op jit(solution)/shard_map/bhqk,bqhd->bkhd/dot_general | solution.py:70
  275.5 5.1 all-to-all-start.12
  306.4 5.8 %all-to-all-start.7 = ((bf16[1,64,1,8,384]{4,3,2,0,1:T(8,128)(2,1)}), bf16[1,64,1,8,384]{4,3,2,0,1:T(8,128)(2,1)S(1)}, u32[]{:S(2)}, u32[]{:S(2)}) async-start(bf16[1,64,1,8,384]{4,3,2,0,1:T(8,128)(2,1)} %copy.229), calls=%async_computation.7 | async-start | bytes 786432 | tf_op jit(solution)/shard_map/all_to_all | solution.py:233
  315.6 5.6 %all-to-all-done.7 = bf16[1,64,1,8,384]{4,3,2,0,1:T(8,128)(2,1)S(1)} async-done(((bf16[1,64,1,8,384]{4,3,2,0,1:T(8,128)(2,1)}), bf16[1,64,1,8,384]{4,3,2,0,1:T(8,128)(2,1)S(1)}, u32[]{:S(2)}, u32[]{:S(2)}) %all-to-all-start.7) | async-done | bytes 393248 | tf_op jit(solution)/shard_map/all_to_all | solution.py:233
  321.3 5.1 all-to-all-start.3
  326.5 7.4 %all-to-all-done.3 = bf16[1,2,256,384]{3,1,0,2:T(2,128)(2,1)S(1)} async-done(((bf16[1,2,256,384]{3,1,0,2:T(2,128)(2,1)}), bf16[1,2,256,384]{3,1,0,2:T(2,128)(2,1)S(1)}, u32[]{:S(2)}, u32[]{:S(2)}) %all-to-all-start.3) | async-done | bytes 393248 | tf_op jit(solution)/shard_map/all_to_all | solution.py:211
  335.8 3.1 reduce-scatter.4.cloned.1.call-done
  347.3 5.4 bitcast_convert_fusion
  354.7 9.3 %all-reduce = bf16[768]{0:T(1024)(128)(2,1)S(1)} all-reduce(bf16[768]{0:T(1024)(128)(2,1)S(1)} %get-tuple-element.7), channel_id=5, replica_groups=mesh['dp'=4,'fy'=4,'fx'=8] {'dp'}, use_global_device_ids=true, to_apply=%region_19.20.clone | all-reduce | flops 768 | bytes 3072
  364.1 64.7 %psum.50 = bf16[192]{0:T(256)(128)(2,1)S(1)} all-reduce(bf16[192]{0:T(256)(128)(2,1)S(1)} %dynamic-slice.1), channel_id=1, replica_groups=mesh['dp'=4,'fy'=4,'fx'=8] {'fy','fx'}, use_global_device_ids=true, to_apply=%region_18.19 | all-reduce | flops 192 | bytes 768 | tf_op jit(solution)/shard_map/psum | solution.py:340
  429.4 2.9 fusion.23
  435.0 10.8 %psum.46 = f32[3,768]{1,0:T(4,128)S(1)} all-reduce(f32[3,768]{1,0:T(4,128)S(1)} %multiply_reduce_fusion.4), channel_id=1, replica_groups=mesh['dp'=4,'fy'=4,'fx'=8] {'dp'}, use_global_device_ids=true, to_apply=%region_21.22 | all-reduce | flops 2304 | bytes 18432 | tf_op jit(solution)/shard_map/psum | solution.py:336
  445.8 23.7 %psum.47 = f32[3,768]{1,0:T(4,128)S(1)} all-reduce(f32[3,768]{1,0:T(4,128)S(1)} %psum.46), channel_id=1, replica_groups=mesh['dp'=4,'fy'=4,'fx'=8] {'fx'}, use_global_device_ids=true, to_apply=%region_22.23 | all-reduce | flops 2304 | bytes 18432 | tf_op jit(solution)/shard_map/psum | solution.py:336
  470.1 70.0 %all-reduce.7.cloned.1.call-done = (bf16[192,2304]{1,0:T(8,128)(2,1)}, bf16[192,768]{1,0:T(8,128)(2,1)}) async-done(((bf16[192,2304]{1,0:T(8,128)(2,1)}, bf16[192,768]{1,0:T(8,128)(2,1)}), (bf16[192,2304]{1,0:T(8,128)(2,1)}, bf16[192,768]{1,0:T(8,128)(2,1)})) %all-reduce.7.cloned.1.call-update) | async-done | bytes 1179664 | tf_op jit(solution)/shard_map/psum | solution.py:338
  (170 shorter events, 111.5 us)
Async XLA Ops:
  8.0 55.0 %copy-start = (bf16[768,2304]{1,0:T(8,128)(2,1)S(1)}, bf16[768,2304]{1,0:T(8,128)(2,1)}, u32[]{:S(2)}) copy-start(bf16[768,2304]{1,0:T(8,128)(2,1)} %param.15) | copy-start | bytes 10616836
  10.5 8.3 %copy-start.23 = (s32[1,16,8]{1,2,0:T(8,128)S(1)}, s32[1,16,8]{1,2,0:T(8,128)}, u32[]{:S(2)}) copy-start(s32[1,16,8]{1,2,0:T(8,128)} %param.10) | copy-start | bytes 1540
  10.5 8.9 %copy-start.27 = (s32[1,64]{1,0:T(1,128)S(1)}, s32[1,64]{1,0:T(1,128)}, u32[]{:S(2)}) copy-start(s32[1,64]{1,0:T(1,128)} %param.12) | copy-start | bytes 772
  12.2 54.9 %all-to-all-start.10 = ((bf16[1,16,4,8,384]{4,3,1,0,2:T(8,128)(2,1)}), bf16[1,16,4,8,384]{4,3,1,0,2:T(8,128)(2,1)}, u32[]{:S(2)}, u32[]{:S(2)}) async-start(bf16[1,16,4,8,384]{4,3,1,0,2:T(8,128)(2,1)} %copy.239), calls=%async_computation.10 | async-start | bytes 786432 | tf_op jit(solution)/shard_map/all_to_all | solution.py:273
  59.2 2.1 copy-start.2
  59.2 2.3 copy-start.12
  59.2 2.3 copy-start.25
  62.9 2.0 copy-start.21
  67.1 18.8 %all-to-all-start.6 = ((bf16[1,16,4,8,384]{4,3,1,0,2:T(8,128)(2,1)}), bf16[1,16,4,8,384]{4,3,1,0,2:T(8,128)(2,1)}, u32[]{:S(2)}, u32[]{:S(2)}) async-start(bf16[1,16,4,8,384]{4,3,1,0,2:T(8,128)(2,1)} %copy.224), calls=%async_computation.6 | async-start | bytes 786432 | tf_op jit(solution)/shard_map/all_to_all | solution.py:218
  85.9 13.1 %all-to-all-start.5 = ((bf16[1,16,4,8,384]{4,3,1,0,2:T(8,128)(2,1)}), bf16[1,16,4,8,384]{4,3,1,0,2:T(8,128)(2,1)}, u32[]{:S(2)}, u32[]{:S(2)}) async-start(bf16[1,16,4,8,384]{4,3,1,0,2:T(8,128)(2,1)} %copy.223), calls=%async_computation.5 | async-start | bytes 786432 | tf_op jit(solution)/shard_map/all_to_all | solution.py:215
  99.0 25.0 %copy-start.14 = (bf16[1,16,32,384]{3,2,1,0:T(8,128)(2,1)S(1)}, bf16[1,16,32,384]{3,2,1,0:T(8,128)(2,1)}, u32[]{:S(2)}) copy-start(bf16[1,16,32,384]{3,2,1,0:T(8,128)(2,1)} %get-tuple-element.15) | copy-start | bytes 1179652
  134.2 25.2 %all-to-all-start.1 = ((bf16[8,2,32,384]{3,2,1,0:T(8,128)(2,1)}), bf16[8,2,32,384]{3,2,1,0:T(8,128)(2,1)}, u32[]{:S(2)}, u32[]{:S(2)}) async-start(bf16[8,2,32,384]{3,2,1,0:T(8,128)(2,1)} %bitcast.250), calls=%async_computation.1 | async-start | bytes 786432 | tf_op jit(solution)/shard_map/all_to_all | solution.py:193
  159.4 16.3 %all-to-all-start = ((bf16[8,2,32,384]{3,2,1,0:T(8,128)(2,1)}), bf16[8,2,32,384]{3,2,1,0:T(8,128)(2,1)}, u32[]{:S(2)}, u32[]{:S(2)}) async-start(bf16[8,2,32,384]{3,2,1,0:T(8,128)(2,1)} %bitcast.249), calls=%async_computation | async-start | bytes 786432 | tf_op jit(solution)/shard_map/all_to_all | solution.py:199
  175.7 42.6 %all-to-all-start.11 = ((bf16[1,64,1,8,384]{4,3,2,0,1:T(8,128)(2,1)}), bf16[1,64,1,8,384]{4,3,2,0,1:T(8,128)(2,1)}, u32[]{:S(2)}, u32[]{:S(2)}) async-start(bf16[1,64,1,8,384]{4,3,2,0,1:T(8,128)(2,1)} %copy.244), calls=%async_computation.11 | async-start | bytes 786432 | tf_op jit(solution)/shard_map/all_to_all | solution.py:291
  218.3 12.9 %all-to-all-start.13 = ((bf16[1,64,1,8,384]{4,3,2,0,1:T(8,128)(2,1)}), bf16[1,64,1,8,384]{4,3,2,0,1:T(8,128)(2,1)}, u32[]{:S(2)}, u32[]{:S(2)}) async-start(bf16[1,64,1,8,384]{4,3,2,0,1:T(8,128)(2,1)} %copy.253), calls=%async_computation.13 | async-start | bytes 786432 | tf_op jit(solution)/shard_map/all_to_all | solution.py:292
  231.2 13.1 %all-to-all-start.15 = ((bf16[1,64,1,8,384]{4,3,2,0,1:T(8,128)(2,1)}), bf16[1,64,1,8,384]{4,3,2,0,1:T(8,128)(2,1)}, u32[]{:S(2)}, u32[]{:S(2)}) async-start(bf16[1,64,1,8,384]{4,3,2,0,1:T(8,128)(2,1)} %copy.262), calls=%async_computation.15 | async-start | bytes 786432 | tf_op jit(solution)/shard_map/all_to_all | solution.py:293
  244.3 17.6 %all-to-all-start.14 = ((bf16[1,2,256,384]{3,1,0,2:T(2,128)(2,1)}), bf16[1,2,256,384]{3,1,0,2:T(2,128)(2,1)}, u32[]{:S(2)}, u32[]{:S(2)}) async-start(bf16[1,2,256,384]{3,1,0,2:T(2,128)(2,1)} %copy.257), calls=%async_computation.14 | async-start | bytes 786432 | tf_op jit(solution)/shard_map/all_to_all | solution.py:262
  261.8 13.7 %all-to-all-start.9 = ((bf16[1,2,256,384]{3,1,0,2:T(2,128)(2,1)}), bf16[1,2,256,384]{3,1,0,2:T(2,128)(2,1)}, u32[]{:S(2)}, u32[]{:S(2)}) async-start(bf16[1,2,256,384]{3,1,0,2:T(2,128)(2,1)} %copy.236), calls=%async_computation.9 | async-start | bytes 786432 | tf_op jit(solution)/shard_map/all_to_all | solution.py:260
  275.5 16.3 %all-to-all-start.12 = ((bf16[1,2,256,384]{3,1,0,2:T(2,128)(2,1)}), bf16[1,2,256,384]{3,1,0,2:T(2,128)(2,1)}, u32[]{:S(2)}, u32[]{:S(2)}) async-start(bf16[1,2,256,384]{3,1,0,2:T(2,128)(2,1)} %copy.248), calls=%async_computation.12 | async-start | bytes 786432 | tf_op jit(solution)/shard_map/all_to_all | solution.py:261
  280.6 58.3 %reduce-scatter.4.cloned.1.call-start = ((), (), s32[]{:S(2)}) async-start(), calls=%async_computation.19 | async-start | bytes 884736 | tf_op jit(solution)/shard_map/reduce_scatter | solution.py:330
  291.8 1.2 copy-start.9
  291.8 1.3 copy-start.17
  292.9 1.1 copy-start.16
  293.0 1.1 copy-start.7
  293.0 1.2 copy-start.5
  293.0 1.2 copy-start.15
  293.1 1.7 copy-start.4
  293.1 1.7 copy-start.26
  294.8 2.2 copy-start.19
  301.7 1.5 copy-start.11
  301.7 1.5 copy-start.24
  305.3 6.9 %copy-start.18 = (bf16[2,256,6,64]{1,3,2,0:T(8,128)(2,1)S(1)}, bf16[2,256,6,64]{1,3,2,0:T(8,128)(2,1)}, u32[]{:S(2)}) copy-start(bf16[2,256,6,64]{1,3,2,0:T(8,128)(2,1)} %reshape.443) | copy-start | bytes 1179652
  305.3 6.9 %copy-start.29 = (f32[2,6,256]{2,1,0:T(8,128)S(1)}, f32[2,6,256]{2,1,0:T(8,128)}, u32[]{:S(2)}) copy-start(f32[2,6,256]{2,1,0:T(8,128)} %get-tuple-element.27) | copy-start | bytes 36868
  306.4 14.9 %all-to-all-start.7 = ((bf16[1,64,1,8,384]{4,3,2,0,1:T(8,128)(2,1)}), bf16[1,64,1,8,384]{4,3,2,0,1:T(8,128)(2,1)S(1)}, u32[]{:S(2)}, u32[]{:S(2)}) async-start(bf16[1,64,1,8,384]{4,3,2,0,1:T(8,128)(2,1)} %copy.229), calls=%async_computation.7 | async-start | bytes 786432 | tf_op jit(solution)/shard_map/all_to_all | solution.py:233
  315.6 18.3 %copy-start.20 = (bf16[1,16,32,768]{3,2,1,0:T(8,128)(2,1)S(1)}, bf16[1,16,32,768]{3,2,1,0:T(8,128)(2,1)}, u32[]{:S(2)}) copy-start(bf16[1,16,32,768]{3,2,1,0:T(8,128)(2,1)} %param.17) | copy-start | bytes 2359300
  321.3 12.6 %all-to-all-start.3 = ((bf16[1,2,256,384]{3,1,0,2:T(2,128)(2,1)}), bf16[1,2,256,384]{3,1,0,2:T(2,128)(2,1)S(1)}, u32[]{:S(2)}, u32[]{:S(2)}) async-start(bf16[1,2,256,384]{3,1,0,2:T(2,128)(2,1)} %copy.219), calls=%async_computation.3 | async-start | bytes 786432 | tf_op jit(solution)/shard_map/all_to_all | solution.py:211
  326.4 105.9 %all-reduce.5.cloned.1.call-start = ((), (), s32[]{:S(2)}) async-start(), calls=%async_computation.20 | async-start | bytes 196608 | tf_op jit(solution)/shard_map/psum | solution.py:333
  334.0 5.0 copy-start.10
  335.8 6.1 %copy-start.8 = (bf16[8,1,2,32,384]{4,3,2,0,1:T(8,128)(2,1)S(1)}, bf16[8,1,2,32,384]{4,3,2,0,1:T(8,128)(2,1)}, u32[]{:S(2)}) copy-start(bf16[8,1,2,32,384]{4,3,2,0,1:T(8,128)(2,1)} %copy-done.7) | copy-start | bytes 1179652
  338.9 95.0 %reduce-scatter.8.cloned.1.call-start = ((), (), s32[]{:S(2)}) async-start(), calls=%async_computation.22 | async-start | bytes 1474560 | tf_op jit(solution)/shard_map/reduce_scatter | solution.py:346
  339.8 4.8 copy-start.6
  339.8 94.0 %reduce-scatter.6.cloned.1.call-start = ((), (), s32[]{:S(2)}) async-start(), calls=%async_computation.21 | async-start | bytes 4423680 | tf_op jit(solution)/shard_map/reduce_scatter | solution.py:343
  341.9 5.4 copy-start.22
  352.8 0.7 copy-start.28
  352.8 76.6 %copy-start.3 = (f32[1,16,32,768]{3,2,1,0:T(8,128)S(1)}, f32[1,16,32,768]{3,2,1,0:T(8,128)}, u32[]{:S(2)}) copy-start(f32[1,16,32,768]{3,2,1,0:T(8,128)} %broadcast_in_dim.39) | copy-start | bytes 4718596
  352.8 76.6 %copy-start.13 = (bf16[1,16,32,768]{3,2,1,0:T(8,128)(2,1)S(1)}, bf16[1,16,32,768]{3,2,1,0:T(8,128)(2,1)}, u32[]{:S(2)}) copy-start(bf16[1,16,32,768]{3,2,1,0:T(8,128)(2,1)} %param.9) | copy-start | bytes 2359300
  352.8 187.4 %all-reduce.7.cloned.1.call-start = ((), (), s32[]{:S(2)}) async-start(), calls=%async_computation.23 | async-start | bytes 2359296 | tf_op jit(solution)/shard_map/psum | solution.py:338
  540.2 4.5 copy-start.1
Sparse Core Ops, SparseCore 0:
  302.8 36.0 reduce-scatter.3
  341.4 45.4 all-reduce.4
Sparse Core Ops, SparseCore 1:
  342.4 26.8 reduce-scatter.7
  371.5 42.9 reduce-scatter.5
  434.0 106.1 all-reduce.6
